TPU v7x, 256 devices: a whole 4x4x8 slice. The times are simulated.
256 devices in a mesh: seq: 32 (over x, y, core), head: 8 (over z).
Axes of the slice: x: 4, y: 4, z: 8, core: 2. Of those that a mesh axis runs over, the one named last changes fastest.
Arguments:
- query_rows: bfloat16 [4096, 3072], P('seq', 'head'), may hold values from -30 to 30
- key_rows: bfloat16 [4096, 3072], P('seq', 'head'), may hold values from -22.5 to 22.5
- value_rows: bfloat16 [4096, 3072], P('seq', 'head'), may hold values from -6 to 6
- output_grad: bfloat16 [4096, 5120], P('seq', 'head'), may hold values from -6 to 6
- out_weight: bfloat16 [5120, 3072], P(None, 'head'), may hold values from -0.078125 to 0.078125
- clusters: int32 [64], replicated, may hold values from 0 to 3
Outputs:
- query_grad: bfloat16 [4096, 3072], P('seq', 'head')
- key_grad: bfloat16 [4096, 3072], P('seq', 'head')
- value_grad: bfloat16 [4096, 3072], P('seq', 'head')
Inputs may be any that keep to these rules, and one draw needn't show every extreme that they name: `clusters`: cluster of each block of 64 tokens.
All inputs are finite; a program needn't handle non-finite values.
Results may differ from a plain program's by a relative error of at most 0.023.
Values may be sent and summed in bfloat16 or wider, within the bound.
No kernel may reach another device: no remote copies, remote signals or barrier semaphores. Data moves between devices by JAX's collectives and lax.ppermute only.
A program may use at most 64 MiB of HBM per device.

v0:
```python
import jax
import jax.numpy as jnp
from jax import lax
from jax.sharding import PartitionSpec as P

HS = 128
BLK = 64


def shards(query_rows, key_rows, value_rows, output_grad, out_weight, clusters):
    rows_here = query_rows.shape[0]
    columns = query_rows.shape[1]
    heads_here = columns // HS
    score_scale = HS ** (-0.5)
    all_rows = rows_here * lax.axis_size("seq")
    block_count = clusters.shape[0]
    local_blocks = rows_here // BLK
    tile_blocks = min(max(512 // BLK, 1), block_count)
    tile_rows = tile_blocks * BLK
    full_grad = lax.all_gather(output_grad, "head", axis=1, tiled=True)
    grad_attended = jnp.dot(full_grad, out_weight, preferred_element_type=jnp.float32).astype(
        jnp.bfloat16
    )
    keys_all, values_all = (
        lax.all_gather(key_rows, "seq", axis=0, tiled=True),
        lax.all_gather(value_rows, "seq", axis=0, tiled=True),
    )
    query_split = query_rows.reshape(rows_here, heads_here, HS)
    grad_split = grad_attended.reshape(rows_here, heads_here, HS)
    key_blocks = keys_all.reshape(block_count, BLK, columns)
    value_blocks = values_all.reshape(block_count, BLK, columns)
    block_ids = jnp.arange(block_count, dtype=jnp.int32)
    first_block = lax.axis_index("seq") * local_blocks

    def block_list(local):
        query_block = first_block + local
        usable = (clusters == clusters[query_block]) & (block_ids <= query_block)
        order = jnp.argsort(jnp.where(usable, block_ids, block_count + block_ids))
        padded = jnp.concatenate([order, jnp.zeros((tile_blocks,), jnp.int32)])
        return (padded, jnp.sum(usable.astype(jnp.int32)), query_block)

    lists, counts, query_blocks = jax.vmap(block_list)(jnp.arange(local_blocks, dtype=jnp.int32))

    def tile_data(local, turn):
        picked = lax.dynamic_slice_in_dim(lists[local], turn * tile_blocks, tile_blocks, 0)
        tile_keys = key_blocks[picked].reshape(tile_rows, heads_here, HS)
        tile_values = value_blocks[picked].reshape(tile_rows, heads_here, HS)
        slot_ok = turn * tile_blocks + jnp.arange(tile_blocks, dtype=jnp.int32) < counts[local]
        key_pos = (picked[:, None] * BLK + jnp.arange(BLK, dtype=jnp.int32)[None, :]).reshape(
            tile_rows
        )
        query_pos = query_blocks[local] * BLK + jnp.arange(BLK, dtype=jnp.int32)
        permitted = jnp.repeat(slot_ok, BLK)[None, :] & (key_pos[None, :] <= query_pos[:, None])
        return (picked, tile_keys, tile_values, permitted)

    def tile_scores(query_block, tile_keys, permitted):
        scores = (
            jnp.einsum("qhd,khd->hqk", query_block, tile_keys, preferred_element_type=jnp.float32)
            * score_scale
        )
        return jnp.where(permitted[None], scores, -jnp.inf)

    def one_block(local, state):
        query_out, log_out, corr_out, key_buffer, value_buffer = state
        query_block = lax.dynamic_slice_in_dim(query_split, local * BLK, BLK, 0)
        grad_block = lax.dynamic_slice_in_dim(grad_split, local * BLK, BLK, 0)
        turns = (counts[local] + tile_blocks - 1) // tile_blocks

        def first_pass(turn, carry):
            running_max, running_total = carry
            picked, tile_keys, tile_values, permitted = tile_data(local, turn)
            scores = tile_scores(query_block, tile_keys, permitted)
            new_max = jnp.maximum(running_max, jnp.max(scores, axis=2))
            running_total = running_total * jnp.exp(running_max - new_max) + jnp.sum(
                jnp.exp(scores - new_max[:, :, None]), axis=2
            )
            return (new_max, running_total)

        start_max = jnp.full((heads_here, BLK), -jnp.inf, jnp.float32)
        start_total = jnp.zeros((heads_here, BLK), jnp.float32)
        row_max, row_total = lax.fori_loop(0, turns, first_pass, (start_max, start_total))
        log_total = row_max + jnp.log(row_total)

        def second_pass(turn, running):
            picked, tile_keys, tile_values, permitted = tile_data(local, turn)
            scores = tile_scores(query_block, tile_keys, permitted)
            probability_b = jnp.exp(scores - log_total[:, :, None]).astype(jnp.bfloat16)
            return running + jnp.einsum(
                "hqk,khd->qhd", probability_b, tile_values, preferred_element_type=jnp.float32
            )

        attended = lax.fori_loop(
            0, turns, second_pass, jnp.zeros((BLK, heads_here, HS), jnp.float32)
        ).astype(jnp.bfloat16)
        correction = jnp.sum(grad_block.astype(jnp.float32) * attended.astype(jnp.float32), axis=2)

        def third_pass(turn, carry):
            query_acc, key_acc, value_acc = carry
            picked, tile_keys, tile_values, permitted = tile_data(local, turn)
            scores = tile_scores(query_block, tile_keys, permitted)
            probability = jnp.exp(scores - log_total[:, :, None])
            grad_prob = jnp.einsum(
                "qhd,khd->hqk", grad_block, tile_values, preferred_element_type=jnp.float32
            )
            grad_score = (
                probability * (grad_prob - correction.T[:, :, None]) * score_scale
            ).astype(jnp.bfloat16)
            query_acc = query_acc + jnp.einsum(
                "hqk,khd->qhd", grad_score, tile_keys, preferred_element_type=jnp.float32
            )
            key_term = jnp.einsum(
                "hqk,qhd->khd", grad_score, query_block, preferred_element_type=jnp.float32
            )
            value_term = jnp.einsum(
                "hqk,qhd->khd",
                probability.astype(jnp.bfloat16),
                grad_block,
                preferred_element_type=jnp.float32,
            )
            key_acc = key_acc.at[picked].add(key_term.reshape(tile_blocks, BLK, columns))
            value_acc = value_acc.at[picked].add(value_term.reshape(tile_blocks, BLK, columns))
            return (query_acc, key_acc, value_acc)

        query_acc, key_buffer, value_buffer = lax.fori_loop(
            0,
            turns,
            third_pass,
            (jnp.zeros((BLK, heads_here, HS), jnp.float32), key_buffer, value_buffer),
        )
        query_out = lax.dynamic_update_slice_in_dim(
            query_out, query_acc.reshape(BLK, columns).astype(jnp.bfloat16), local * BLK, 0
        )
        log_out = lax.dynamic_update_slice_in_dim(log_out, log_total.T, local * BLK, 0)
        corr_out = lax.dynamic_update_slice_in_dim(corr_out, correction, local * BLK, 0)
        return (query_out, log_out, corr_out, key_buffer, value_buffer)

    start = (
        jnp.zeros((rows_here, columns), jnp.bfloat16),
        jnp.zeros((rows_here, heads_here), jnp.float32),
        jnp.zeros((rows_here, heads_here), jnp.float32),
        jnp.zeros((block_count, BLK, columns), jnp.float32),
        jnp.zeros((block_count, BLK, columns), jnp.float32),
    )
    query_grad, log_rows, correction, key_buffer, value_buffer = lax.fori_loop(
        0, local_blocks, one_block, start
    )
    joined = jnp.concatenate(
        [key_buffer.reshape(all_rows, columns), value_buffer.reshape(all_rows, columns)], axis=1
    )
    summed = lax.psum_scatter(
        joined.astype(jnp.bfloat16), "seq", scatter_dimension=0, tiled=True
    ).astype(jnp.float32)
    key_grad = summed[:, :columns].astype(jnp.bfloat16)
    value_grad = summed[:, columns:].astype(jnp.bfloat16)
    return (query_grad, key_grad, value_grad)


def solution(mesh):
    return jax.shard_map(
        shards,
        mesh=mesh,
        in_specs=(
            P("seq", "head"),
            P("seq", "head"),
            P("seq", "head"),
            P("seq", "head"),
            P(None, "head"),
            P(),
        ),
        out_specs=(P("seq", "head"), P("seq", "head"), P("seq", "head")),
        check_vma=False,
    )
```

profile of v0, /device:TPU:2, one launch (start us, length us, event | category | flops | bytes accessed | tf_op | source)
XLA Modules:
  0.0 414.0 jit_solution(17297681794545578149)
XLA Ops:
  13.8 38.3 %all-gather.6.cloned.1.call-done = bf16[128,5120]{1,0:T(8,128)(2,1)} async-done(((bf16[128,640]{1,0:T(8,128)(2,1)}), bf16[128,5120]{1,0:T(8,128)(2,1)}) %all-gather.6.cloned.1.call-update) | async-done | bytes 1310736 | tf_op jit(solution)/shard_map/all_gather | solution.py:20
  52.1 3.4 convolution_convert_fusion
  55.7 46.5 %all-gather.4.cloned.1.call-done = bf16[4096,384]{1,0:T(8,128)(2,1)} async-done(((bf16[128,384]{1,0:T(8,128)(2,1)}), bf16[4096,384]{1,0:T(8,128)(2,1)}) %all-gather.4.cloned.1.call-update) | async-done | bytes 3145744 | tf_op jit(solution)/shard_map/all_gather | solution.py:25
  102.3 51.9 %all-gather.8.cloned.1.call-done = bf16[4096,384]{1,0:T(8,128)(2,1)} async-done(((bf16[128,384]{1,0:T(8,128)(2,1)}), bf16[4096,384]{1,0:T(8,128)(2,1)}) %all-gather.8.cloned.1.call-update) | async-done | bytes 3145744 | tf_op jit(solution)/shard_map/all_gather | solution.py:26
  154.1 3.4 broadcast.357.clone
  157.6 3.4 broadcast.357
  161.0 60.6 %while.160 = (s32[]{:T(128)}, bf16[128,384]{1,0:T(8,128)(2,1)S(1)}, f32[64,64,384]{2,1,0:T(8,128)}, f32[64,64,384]{2,1,0:T(8,128)}, s32[2]{0:T(128)S(1)}, /*inde...) while((s32[]{:T(128)}, bf16[128,384]{1,0:T(8,128)(2,1)S(1)}, ...), condition=%wide.region_14.15_spmd, body=%wide.region_2.14_spmd.sunk | while | flops 203789568 | bytes 27048524 | solution.py:144
  163.6 4.5 %while.161 = (s32[]{:T(128)}, f32[3,64]{1,0:T(4,128)S(1)}, f32[3,64]{1,0:T(4,128)S(1)}, s32[]{:T(128)}, s32[1]{0:T(128)}, /*index=5*/s32[2,72]{1,0:T(2,128)S(1)}...) while((s32[]{:T(128)}, f32[3,64]{1,0:T(4,128)S(1)}, ...), condition=%wide.region_6.6_spmd, body=%wide.region_3.5_spmd.sunk | while | flops 25724920 | bytes 2892503 | solution.py:81
  164.8 2.5 gather_fusion
  168.1 7.0 %while.162 = (s32[]{:T(128)}, f32[64,3,128]{2,0,1:T(8,128)S(1)}, s32[]{:T(128)}, s32[2,72]{1,0:T(2,128)S(1)}, s32[]{:T(128)}, /*index=5*/bf16[64,64,384]{2,1,0:T...) while((s32[]{:T(128)}, f32[64,3,128]{2,0,1:T(8,128)S(1)}, ...), condition=%wide.region_8.8_spmd, body=%wide.region_7.7_spmd.sunk | while | flops 50816632 | bytes 4259583 | solution.py:92
  169.4 2.5 gather_fusion.2
  172.1 2.5 gather_fusion.1
  175.3 16.0 %while.163 = (s32[]{:T(128)}, f32[64,3,128]{2,0,1:T(8,128)S(1)}, f32[64,64,384]{2,1,0:T(8,128)}, f32[64,64,384]{2,1,0:T(8,128)}, s32[]{:T(128)}, /*index=5*/s32[...) while((s32[]{:T(128)}, f32[64,3,128]{2,0,1:T(8,128)S(1)}, ...), condition=%wide.region_13.13_spmd, body=%wide.region_10.12_spmd.sunk | while | flops 127100536 | bytes 19153504 | solution.py:124
  176.5 2.5 gather_fusion.4
  185.2 3.0 scatter_fusion
  188.2 3.1 scatter_fusion.1
  193.9 4.5 %while.161 = (s32[]{:T(128)}, f32[3,64]{1,0:T(4,128)S(1)}, f32[3,64]{1,0:T(4,128)S(1)}, s32[]{:T(128)}, s32[1]{0:T(128)}, /*index=5*/s32[2,72]{1,0:T(2,128)S(1)}...) while((s32[]{:T(128)}, f32[3,64]{1,0:T(4,128)S(1)}, ...), condition=%wide.region_6.6_spmd, body=%wide.region_3.5_spmd.sunk | while | flops 25724920 | bytes 2892503 | solution.py:81
  198.5 7.0 %while.162 = (s32[]{:T(128)}, f32[64,3,128]{2,0,1:T(8,128)S(1)}, s32[]{:T(128)}, s32[2,72]{1,0:T(2,128)S(1)}, s32[]{:T(128)}, /*index=5*/bf16[64,64,384]{2,1,0:T...) while((s32[]{:T(128)}, f32[64,3,128]{2,0,1:T(8,128)S(1)}, ...), condition=%wide.region_8.8_spmd, body=%wide.region_7.7_spmd.sunk | while | flops 50816632 | bytes 4259583 | solution.py:92
  205.6 16.0 %while.163 = (s32[]{:T(128)}, f32[64,3,128]{2,0,1:T(8,128)S(1)}, f32[64,64,384]{2,1,0:T(8,128)}, f32[64,64,384]{2,1,0:T(8,128)}, s32[]{:T(128)}, /*index=5*/s32[...) while((s32[]{:T(128)}, f32[64,3,128]{2,0,1:T(8,128)S(1)}, ...), condition=%wide.region_13.13_spmd, body=%wide.region_10.12_spmd.sunk | while | flops 127100536 | bytes 19153504 | solution.py:124
  215.5 3.1 scatter_fusion
  218.5 3.1 scatter_fusion.1
  221.6 3.5 convert.11
  226.8 3.2 pad_maximum_fusion
  230.0 175.9 %reduce-scatter.2.cloned.1.call-done = bf16[128,768]{1,0:T(8,128)(2,1)} async-done(((bf16[4096,768]{1,0:T(8,128)(2,1)}), bf16[128,768]{1,0:T(8,128)(2,1)}) %reduce-scatter.2.cloned.1.call-update) | async-done | bytes 196624 | tf_op jit(solution)/shard_map/reduce_scatter | solution.py:150
  (157 shorter events, 45.1 us)
Async XLA Ops:
  7.2 44.9 %all-gather.6.cloned.1.call-start = ((), (), s32[]{:S(2)}) async-start(), calls=%async_computation.2 | async-start | bytes 1474560 | tf_op jit(solution)/shard_map/all_gather | solution.py:20
  7.9 94.4 %all-gather.4.cloned.1.call-start = ((), (), s32[]{:S(2)}) async-start(), calls=%async_computation.1 | async-start | bytes 3244032 | tf_op jit(solution)/shard_map/all_gather | solution.py:25
  8.6 145.5 %all-gather.8.cloned.1.call-start = ((), (), s32[]{:S(2)}) async-start(), calls=%async_computation.3 | async-start | bytes 3244032 | tf_op jit(solution)/shard_map/all_gather | solution.py:26
  9.4 396.5 %reduce-scatter.2.cloned.1.call-start = ((), (), s32[]{:S(2)}) async-start(), calls=%async_computation.4 | async-start | bytes 6488064 | tf_op jit(solution)/shard_map/reduce_scatter | solution.py:150
  221.6 5.2 %copy-start.1 = (bf16[128,384]{1,0:T(8,128)(2,1)}, bf16[128,384]{1,0:T(8,128)(2,1)S(1)}, u32[]{:S(2)}) copy-start(bf16[128,384]{1,0:T(8,128)(2,1)S(1)} %get-tuple-element.874) | copy-start | bytes 294916
  221.6 4.6 %copy-start = (f32[64,64,384]{2,1,0:T(8,128)S(1)}, f32[64,64,384]{2,1,0:T(8,128)}, u32[]{:S(2)}) copy-start(f32[64,64,384]{2,1,0:T(8,128)} %get-tuple-element.879) | copy-start | bytes 18874372
Sparse Core Ops, SparseCore 0:
  9.8 42.2 all-gather.5
  54.6 47.5 all-gather.3
  104.8 49.2 all-gather.7
  230.1 175.6 reduce-scatter.1
where the time goes:
time: 416 us; the launch traced here: 414 us
  waiting for transfers between devices  315 us (76%)
  local copies, waits for them, and re-layouts  46.6 us (11%)
  other arithmetic  27.7 us (7%)
  between operations  13.9 us (3%)
  matrix products  7.66 us (2%)
    reduce_scatter x1, waiting for transfers between devices, shards(): lax.psum_scatter(joined.astype(jnp.bfloat16), 'seq', scatter_dimension=0,...  176 us
    all_gather x1, waiting for transfers between devices, shards(): lax.all_gather(value_rows, 'seq', axis=0, tiled=True)  51.9 us
    all_gather x1, waiting for transfers between devices, shards(): lax.all_gather(key_rows, 'seq', axis=0, tiled=True)  46.5 us
    all_gather x1, waiting for transfers between devices, shards(): full_grad = lax.all_gather(output_grad, 'head', axis=1, tiled=True)  38.3 us
    gather x6, local copies, waits for them, and re-layouts, tile_data(): tile_keys = key_blocks[picked].reshape(tile_rows, heads_here, HS)  15.1 us
    gather x4, local copies, waits for them, and re-layouts, tile_data(): tile_values = value_blocks[picked].reshape(tile_rows, heads_here, HS)  10.1 us
  transfers between devices with their start and end apart: 4, of which 4 were waited for; matrix products, arithmetic and copies ran while one was open for 2% of the time, Pallas kernels for 0%

commit v1 on v0

--- a/solution.py
+++ b/solution.py
@@ -22,7 +22,9 @@
         jnp.bfloat16
     )
     keys_all, values_all = (
-        lax.all_gather(key_rows, "seq", axis=0, tiled=True),
+        jnp.concatenate(
+            lax.all_to_all(jnp.stack([key_rows] * lax.axis_size("seq")), "seq", 0, 0), axis=0
+        ),
         lax.all_gather(value_rows, "seq", axis=0, tiled=True),
     )
     query_split = query_rows.reshape(rows_here, heads_here, HS)

time: 416 us -> 364 us (0.88)
  waiting for transfers between devices: 315 us -> 254 us
  starting transfers between devices: 0.15 us -> 7.79 us
    all_gather x1 -> x0, waiting for transfers between devices: 46.5 us -> none  [shards(): lax.all_gather(key_rows, 'seq', axis=0, tiled=True)]
    all_gather x1, waiting for transfers between devices: 38.3 us -> 30.3 us  [shards(): full_grad = lax.all_gather(output_grad, 'head', axis=1, tiled=True)]
    all_to_all x0 -> x1, starting transfers between devices: none -> 7.67 us  [shards(): lax.all_to_all(jnp.stack([key_rows] * lax.axis_size('seq')), 'seq', 0, 0)]
    all_gather x1, waiting for transfers between devices: 51.9 us -> 45.7 us  [shards(): lax.all_gather(value_rows, 'seq', axis=0, tiled=True)]
    another operation x10 -> x11, local copies, waits for them, and re-layouts: 6.91 us -> 9.94 us
where the time goes in v1:
time: 364 us; the launch traced here: 362 us
  waiting for transfers between devices  254 us (70%)
  local copies, waits for them, and re-layouts  48.1 us (13%)
  other arithmetic  27.1 us (7%)
  between operations  13.9 us (4%)
  starting transfers between devices  7.79 us (2%)
  matrix products  7.66 us (2%)
    reduce_scatter x1, waiting for transfers between devices, shards(): lax.psum_scatter(joined.astype(jnp.bfloat16), 'seq', scatter_dimension=0,...  176 us
    all_gather x1, waiting for transfers between devices, shards(): lax.all_gather(value_rows, 'seq', axis=0, tiled=True)  45.7 us
    all_gather x1, waiting for transfers between devices, shards(): full_grad = lax.all_gather(output_grad, 'head', axis=1, tiled=True)  30.3 us
    gather x6, local copies, waits for them, and re-layouts, tile_data(): tile_keys = key_blocks[picked].reshape(tile_rows, heads_here, HS)  15.1 us
    gather x4, local copies, waits for them, and re-layouts, tile_data(): tile_values = value_blocks[picked].reshape(tile_rows, heads_here, HS)  10.1 us
    all_to_all x1, starting transfers between devices, shards(): lax.all_to_all(jnp.stack([key_rows] * lax.axis_size('seq')), 'seq', 0, 0)  7.67 us
  transfers between devices with their start and end apart: 4, of which 4 were waited for; matrix products, arithmetic and copies ran while one was open for 2% of the time, Pallas kernels for 0%

profile of v1, /device:TPU:2, one launch (start us, length us, event | category | flops | bytes accessed | tf_op | source)
XLA Modules:
  0.0 362.1 jit_solution(5494485694600730337)
XLA Ops:
  8.7 3.0 stack.2
  11.7 7.7 %all-to-all-start = ((bf16[32,128,384]{2,1,0:T(8,128)(2,1)}), bf16[32,128,384]{2,1,0:T(8,128)(2,1)}, u32[]{:S(2)}, u32[]{:S(2)}) async-start(bf16[32,128,384]{2,1,0:T(8,128)(2,1)} %stack.2), calls=%async_computation | async-start | bytes 6291456 | tf_op jit(solution)/shard_map/all_to_all | solution.py:26
  21.6 30.3 %all-gather.3.cloned.1.call-done = bf16[128,5120]{1,0:T(8,128)(2,1)} async-done(((bf16[128,640]{1,0:T(8,128)(2,1)}), bf16[128,5120]{1,0:T(8,128)(2,1)}) %all-gather.3.cloned.1.call-update) | async-done | bytes 1310736 | tf_op jit(solution)/shard_map/all_gather | solution.py:20
  51.9 3.4 convolution_convert_fusion
  56.5 45.7 %all-gather.5.cloned.1.call-done = bf16[4096,384]{1,0:T(8,128)(2,1)} async-done(((bf16[128,384]{1,0:T(8,128)(2,1)}), bf16[4096,384]{1,0:T(8,128)(2,1)}) %all-gather.5.cloned.1.call-update) | async-done | bytes 3145744 | tf_op jit(solution)/shard_map/all_gather | solution.py:28
  102.2 3.4 broadcast.359.clone
  105.6 3.4 broadcast.359
  109.0 60.6 %while.160 = (s32[]{:T(128)}, bf16[128,384]{1,0:T(8,128)(2,1)S(1)}, f32[64,64,384]{2,1,0:T(8,128)}, f32[64,64,384]{2,1,0:T(8,128)}, s32[2]{0:T(128)S(1)}, /*inde...) while((s32[]{:T(128)}, bf16[128,384]{1,0:T(8,128)(2,1)S(1)}, ...), condition=%wide.region_14.15_spmd, body=%wide.region_2.14_spmd.sunk | while | flops 203789568 | bytes 27048524 | solution.py:146
  111.6 4.5 %while.161 = (s32[]{:T(128)}, f32[3,64]{1,0:T(4,128)S(1)}, f32[3,64]{1,0:T(4,128)S(1)}, s32[]{:T(128)}, s32[1]{0:T(128)}, /*index=5*/s32[2,72]{1,0:T(2,128)S(1)}...) while((s32[]{:T(128)}, f32[3,64]{1,0:T(4,128)S(1)}, ...), condition=%wide.region_6.6_spmd, body=%wide.region_3.5_spmd.sunk | while | flops 25724920 | bytes 2892503 | solution.py:83
  112.9 2.5 gather_fusion
  116.2 7.0 %while.162 = (s32[]{:T(128)}, f32[64,3,128]{2,0,1:T(8,128)S(1)}, s32[]{:T(128)}, s32[2,72]{1,0:T(2,128)S(1)}, s32[]{:T(128)}, /*index=5*/bf16[64,64,384]{2,1,0:T...) while((s32[]{:T(128)}, f32[64,3,128]{2,0,1:T(8,128)S(1)}, ...), condition=%wide.region_8.8_spmd, body=%wide.region_7.7_spmd.sunk | while | flops 50816632 | bytes 4259583 | solution.py:94
  117.4 2.5 gather_fusion.2
  120.1 2.5 gather_fusion.1
  123.3 16.0 %while.163 = (s32[]{:T(128)}, f32[64,3,128]{2,0,1:T(8,128)S(1)}, f32[64,64,384]{2,1,0:T(8,128)}, f32[64,64,384]{2,1,0:T(8,128)}, s32[]{:T(128)}, /*index=5*/s32[...) while((s32[]{:T(128)}, f32[64,3,128]{2,0,1:T(8,128)S(1)}, ...), condition=%wide.region_13.13_spmd, body=%wide.region_10.12_spmd.sunk | while | flops 127100536 | bytes 19153504 | solution.py:126
  133.2 3.0 scatter_fusion
  136.2 3.1 scatter_fusion.1
  141.9 4.5 %while.161 = (s32[]{:T(128)}, f32[3,64]{1,0:T(4,128)S(1)}, f32[3,64]{1,0:T(4,128)S(1)}, s32[]{:T(128)}, s32[1]{0:T(128)}, /*index=5*/s32[2,72]{1,0:T(2,128)S(1)}...) while((s32[]{:T(128)}, f32[3,64]{1,0:T(4,128)S(1)}, ...), condition=%wide.region_6.6_spmd, body=%wide.region_3.5_spmd.sunk | while | flops 25724920 | bytes 2892503 | solution.py:83
  146.5 7.0 %while.162 = (s32[]{:T(128)}, f32[64,3,128]{2,0,1:T(8,128)S(1)}, s32[]{:T(128)}, s32[2,72]{1,0:T(2,128)S(1)}, s32[]{:T(128)}, /*index=5*/bf16[64,64,384]{2,1,0:T...) while((s32[]{:T(128)}, f32[64,3,128]{2,0,1:T(8,128)S(1)}, ...), condition=%wide.region_8.8_spmd, body=%wide.region_7.7_spmd.sunk | while | flops 50816632 | bytes 4259583 | solution.py:94
  153.6 16.0 %while.163 = (s32[]{:T(128)}, f32[64,3,128]{2,0,1:T(8,128)S(1)}, f32[64,64,384]{2,1,0:T(8,128)}, f32[64,64,384]{2,1,0:T(8,128)}, s32[]{:T(128)}, /*index=5*/s32[...) while((s32[]{:T(128)}, f32[64,3,128]{2,0,1:T(8,128)S(1)}, ...), condition=%wide.region_13.13_spmd, body=%wide.region_10.12_spmd.sunk | while | flops 127100536 | bytes 19153504 | solution.py:126
  163.5 3.1 scatter_fusion
  166.6 3.1 scatter_fusion.1
  169.7 3.5 convert.11
  174.8 3.2 pad_maximum_fusion
  178.0 175.9 %reduce-scatter.2.cloned.1.call-done = bf16[128,768]{1,0:T(8,128)(2,1)} async-done(((bf16[4096,768]{1,0:T(8,128)(2,1)}), bf16[128,768]{1,0:T(8,128)(2,1)}) %reduce-scatter.2.cloned.1.call-update) | async-done | bytes 196624 | tf_op jit(solution)/shard_map/reduce_scatter | solution.py:152
  (161 shorter events, 45.7 us)
Async XLA Ops:
  7.2 12.3 %copy-start = (s32[64]{0:T(128)S(1)}, s32[64]{0:T(128)}, u32[]{:S(2)}) copy-start(s32[64]{0:T(128)} %param.19) | copy-start | bytes 772
  7.2 14.2 %copy-start.2 = (bf16[128,384]{1,0:T(8,128)(2,1)S(1)}, bf16[128,384]{1,0:T(8,128)(2,1)}, u32[]{:S(2)}) copy-start(bf16[128,384]{1,0:T(8,128)(2,1)} %param.14) | copy-start | bytes 294916
  7.2 44.7 %all-gather.3.cloned.1.call-start = ((), (), s32[]{:S(2)}) async-start(), calls=%async_computation.2 | async-start | bytes 1474560 | tf_op jit(solution)/shard_map/all_gather | solution.py:20
  7.9 94.2 %all-gather.5.cloned.1.call-start = ((), (), s32[]{:S(2)}) async-start(), calls=%async_computation.3 | async-start | bytes 3244032 | tf_op jit(solution)/shard_map/all_gather | solution.py:28
  11.7 44.8 %all-to-all-start = ((bf16[32,128,384]{2,1,0:T(8,128)(2,1)}), bf16[32,128,384]{2,1,0:T(8,128)(2,1)}, u32[]{:S(2)}, u32[]{:S(2)}) async-start(bf16[32,128,384]{2,1,0:T(8,128)(2,1)} %stack.2), calls=%async_computation | async-start | bytes 6291456 | tf_op jit(solution)/shard_map/all_to_all | solution.py:26
  19.4 334.6 %reduce-scatter.2.cloned.1.call-start = ((), (), s32[]{:S(2)}) async-start(), calls=%async_computation.4 | async-start | bytes 6488064 | tf_op jit(solution)/shard_map/reduce_scatter | solution.py:152
  169.7 5.2 %copy-start.3 = (bf16[128,384]{1,0:T(8,128)(2,1)}, bf16[128,384]{1,0:T(8,128)(2,1)S(1)}, u32[]{:S(2)}) copy-start(bf16[128,384]{1,0:T(8,128)(2,1)S(1)} %get-tuple-element.874) | copy-start | bytes 294916
  169.7 4.6 %copy-start.1 = (f32[64,64,384]{2,1,0:T(8,128)S(1)}, f32[64,64,384]{2,1,0:T(8,128)}, u32[]{:S(2)}) copy-start(f32[64,64,384]{2,1,0:T(8,128)} %get-tuple-element.879) | copy-start | bytes 18874372
Sparse Core Ops, SparseCore 0:
  9.8 42.0 all-gather.2
  54.4 47.6 all-gather.4
  178.1 175.7 reduce-scatter.1
